TPU v7x, 512 devices: a whole 4x8x8 slice. The times are simulated.
512 devices in a mesh: seq: 64 (over z, y_hi, core), head: 8 (over x, y_lo).
Axes of the slice: x: 4, y: 8 (y_hi: 4, y_lo: 2; y = y_hi * 2 + y_lo), z: 8, core: 2. Of those that a mesh axis runs over, the one named last changes fastest.
Arguments:
- block_query_rows: bfloat16 [8192, 5120], P('seq', 'head'), may hold values from -180 to 180
- block_key_rows: bfloat16 [8192, 1024], P('seq', 'head'), may hold values from -6 to 6
- block_value_rows: bfloat16 [8192, 1024], P('seq', 'head'), may hold values from -6 to 6
- stretch_segments: int32 [8192], P('seq'), may hold values from 0 to 15, never falling along the last dimension, each value on 1 to 6144 neighbouring positions
- residual: bfloat16 [8192, 5120], P('seq', 'head'), may hold values from -6 to 6
- out_weight: bfloat16 [5120, 5120], P('head', 'seq'), may hold values from -0.25 to 0.25
- cache_by_prefill: bfloat16 [2, 2, 2048, 16, 1024], P(None, None, 'seq', None, 'head'), may hold values from -6 to 6
- request_pages: int32 [128], replicated, may hold values from 1 to 64, as said below
- request_owner: int32 [128], replicated, may hold values from 0 to 63, as said below
Outputs:
- layer_out: bfloat16 [8192, 5120], P('seq', 'head')
- cache_decode: bfloat16 [2, 2, 4096, 16, 1024], P(None, None, 'seq', None, 'head')
Inputs may be any that keep to these rules, and one draw needn't show every extreme that they name: `stretch_segments`: each request of the block holds at most 6144 tokens, and some request exactly that many. `request_pages`: the requests of one decode device hold at most 64 pages together, and those of some device exactly 64. `request_owner`: never falls along the requests; every device owns at least one request.
All inputs are finite; a program needn't handle non-finite values.
Results may differ from a plain program's by a relative error of at most 0.0065.
Values may be sent and summed in bfloat16 or wider, within the bound.
A program may use at most 128 MiB of HBM per device.

v0:
```python
import jax
import jax.numpy as jnp
from jax import lax
from jax.sharding import PartitionSpec as P

HEAD_SIZE = 128


def on_device(
    block_query_rows,
    block_key_rows,
    block_value_rows,
    stretch_segments,
    residual,
    out_weight,
    cache_by_prefill,
    request_pages,
    request_owner,
):
    seq_count = lax.axis_size("seq")
    seq_place = lax.axis_index("seq")
    rows = block_query_rows.shape[0]
    kv_local = block_key_rows.shape[1] // HEAD_SIZE
    query_groups = block_query_rows.shape[1] // block_key_rows.shape[1]
    query_four = block_query_rows.reshape(rows, kv_local, query_groups, HEAD_SIZE)
    query_place = seq_place * rows + jnp.arange(rows, dtype=jnp.int32)
    scale = HEAD_SIZE ** (-0.5)
    key_part = lax.all_gather(block_key_rows, "seq", axis=0, tiled=True)
    value_part = lax.all_gather(block_value_rows, "seq", axis=0, tiled=True)
    segment_part = lax.all_gather(stretch_segments, "seq", axis=0, tiled=True)
    count = key_part.shape[0]
    key_place = jnp.arange(count, dtype=jnp.int32)
    allowed = (
        (stretch_segments[:, None] == segment_part[None, :])
        & (query_place[:, None] >= key_place[None, :])
        & (key_place[None, :] >= 0)
    )
    running_max = jnp.full((kv_local, query_groups, rows), -1e30, jnp.float32)
    key_three = key_part.reshape(count, kv_local, HEAD_SIZE)
    value_three = value_part.reshape(count, kv_local, HEAD_SIZE)
    scores = (
        jnp.einsum("tkgd,pkd->kgtp", query_four, key_three, preferred_element_type=jnp.float32)
        * scale
    )
    masked = jnp.where(allowed, scores, -1e30)
    new_max = jnp.maximum(running_max, jnp.max(masked, axis=-1))
    weights = jnp.where(allowed, jnp.exp(masked - new_max[..., None]), 0.0)
    new_sum = jnp.sum(weights, axis=-1)
    contribution = jnp.einsum(
        "kgtp,pkd->kgtd",
        weights.astype(jnp.bfloat16),
        value_three,
        preferred_element_type=jnp.float32,
    )
    attention = (
        jnp.transpose(contribution / new_sum[..., None], (2, 0, 1, 3))
        .reshape(rows, -1)
        .astype(jnp.bfloat16)
    )
    partial_value = jnp.dot(
        attention,
        lax.all_gather(out_weight, "seq", axis=1, tiled=True),
        preferred_element_type=jnp.float32,
    )
    feature_width = partial_value.shape[1] // lax.axis_size("head")
    total = lax.psum(partial_value.astype(jnp.bfloat16), "head").astype(jnp.float32)
    mine = lax.dynamic_slice_in_dim(total, lax.axis_index("head") * feature_width, feature_width, 1)
    layer_out = (residual.astype(jnp.float32) + mine).astype(jnp.bfloat16)
    local_pages = cache_by_prefill.shape[2]
    capacity = 2 * local_pages
    per_pair = capacity // seq_count
    owners = jnp.arange(seq_count, dtype=jnp.int32)
    run_pages = jnp.sum(
        jnp.where(request_owner[None, :] == owners[:, None], request_pages[None, :], 0), axis=1
    )
    run_start = jnp.sum(
        jnp.where(request_owner[None, :] < owners[:, None], request_pages[None, :], 0), axis=1
    )
    pair_slots = jnp.arange(per_pair, dtype=jnp.int32)
    offset = (seq_place - run_start) % seq_count
    slot_index = pair_slots[None, :] * seq_count + offset[:, None]
    sending = slot_index < run_pages[:, None]
    local_index = pair_slots[None, :] + ((run_start + offset - seq_place) // seq_count)[:, None]
    local_index = jnp.where(sending, local_index, 0).reshape(-1)
    picked = jnp.take(cache_by_prefill, local_index, axis=2)
    outgoing = jnp.where(
        sending.reshape(-1)[None, None, :, None, None], picked, jnp.zeros_like(picked)
    )
    incoming = lax.all_to_all(outgoing, "seq", split_axis=2, concat_axis=2, tiled=True)
    layers, pair_kv, _, page_len, width = incoming.shape
    arranged = jnp.swapaxes(
        incoming.reshape(layers, pair_kv, seq_count, per_pair, page_len, width), 2, 3
    )
    my_start = run_start[seq_place]
    my_pages = run_pages[seq_place]
    rotated = jnp.roll(arranged, -my_start, axis=3).reshape(
        layers, pair_kv, capacity, page_len, width
    )
    keep = jnp.arange(capacity, dtype=jnp.int32) < my_pages
    cache_decode = jnp.where(keep[None, None, :, None, None], rotated, jnp.zeros_like(rotated))
    return (layer_out, cache_decode)


def solution(mesh):
    return jax.shard_map(
        on_device,
        mesh=mesh,
        in_specs=(
            P("seq", "head"),
            P("seq", "head"),
            P("seq", "head"),
            P("seq"),
            P("seq", "head"),
            P("head", "seq"),
            P(None, None, "seq", None, "head"),
            P(),
            P(),
        ),
        out_specs=(P("seq", "head"), P(None, None, "seq", None, "head")),
        check_vma=False,
    )
```

profile of v0, /device:TPU:16, one launch (start us, length us, event | category | flops | bytes accessed | tf_op | source)
XLA Modules:
  0.0 391.2 jit_solution(16656007094815539979)
XLA Ops:
  7.2 0.7 all-gather.5.cloned.1.call-update
  8.0 1.5 copy.27
  9.5 0.7 all-gather.9.cloned.1.call-update
  10.2 0.8 select_reduce_fusion.1
  11.0 0.8 gather_fusion
  11.9 1.2 select_bitcast_fusion
  13.1 16.5 %all-to-all-start = ((bf16[2,2,64,16,128]{4,3,1,0,2:T(8,128)(2,1)}), bf16[2,2,64,16,128]{4,3,1,0,2:T(8,128)(2,1)S(1)}, u32[]{:S(2)}, u32[]{:S(2)}) async-start(bf16[2,2,64,16,128]{4,3,1,0,2:T(8,128)(2,1)} %select_bitcast_fusion), calls=%async_computation | async-start | bytes 2097152 | tf_op jit(solution)/shard_map/all_to_all | solution.py:89
  29.5 0.0 all-reduce.2.cloned.1.call-start
  29.6 1.1 copy.25
  30.7 98.7 %all-gather = s32[64,1,128]{2,1,0:T(1,128)S(1)} all-gather(s32[1,1,128]{2,1,0:T(1,128)} %bitcast.79), channel_id=1, replica_groups=mesh['seq'=64,'head'=8] {'seq'}, dimensions={0}, use_global_device_ids=true | all-gather | bytes 33280 | tf_op jit(solution)/shard_map/all_gather | solution.py:30
  129.4 4.4 %fusion.7 = pred[128,8192]{0,1:T(8,128)(4,1)S(1)} fusion(s32[128]{0:T(128)S(1)} %iota_add_fusion, s32[128]{0:T(128)} %param.12, s32[8192]{0:T(1024)S(1)} %bitcast.78), kind=kLoop, calls=%fused_computation.11 | loop fusion | flops 3145728 | bytes 1082368 | tf_op jit(solution)/shard_map/and | solution.py:34
  133.8 4.7 %fusion = (f32[5,128]{1,0:T(8,128)S(1)}, f32[8192,128,5]{1,0,2:T(8,128)S(1)}) fusion(pred[128,8192]{0,1:T(8,128)(4,1)S(1)} %fusion.7, bf16[128,5,128]{0,2,1:T(8,128)(2,1)S(1)} %bitcast.76, bf16[8192,128]{1,0:T(8,128)(2,1)} %all-gather.5.cloned.1.call-done), kind=kOutput, calls=%fused_computation.3 | convolution fusion | flops 1357905280 | bytes 24283648 | tf_op jit(solution)/shard_map/tkgd,pkd->kgtp/dot_general | solution.py:42
  138.6 6.9 %copy-done.1 = f32[8192,128,5]{1,0,2:T(8,128)} copy-done((f32[8192,128,5]{1,0,2:T(8,128)}, f32[8192,128,5]{1,0,2:T(8,128)S(1)}, u32[]{:S(2)}) %copy-start.1) | copy-done | bytes 20971544
  145.5 5.2 %fusion.1 = f32[5,128]{1,0:T(8,128)S(1)} fusion(f32[8192,128,5]{1,0,2:T(8,128)S(1)} %get-tuple-element.7, f32[5,128]{1,0:T(8,128)S(1)} %broadcast_maximum_fusion, pred[128,8192]{0,1:T(8,128)(4,1)S(1)} %fusion.7), kind=kLoop, calls=%fused_computation.4 | loop fusion | flops 26213760 | bytes 22025216 | tf_op jit(solution)/shard_map/reduce_sum | solution.py:48
  150.7 40.7 %all-gather.7.cloned.1.call-done = bf16[8192,128]{0,1:T(8,128)(2,1)} async-done(((bf16[128,128]{0,1:T(8,128)(2,1)}), bf16[8192,128]{0,1:T(8,128)(2,1)}) %all-gather.7.cloned.1.call-update) | async-done | bytes 2097168 | tf_op jit(solution)/shard_map/all_gather | solution.py:29
  191.4 12.9 %fusion.16 = bf16[5,128,128]{1,2,0:T(8,128)(2,1)S(1)} fusion(f32[8192,128,5]{1,0,2:T(8,128)} %copy-done.1, f32[5,128]{1,0:T(8,128)S(1)} %broadcast_maximum_fusion, pred[128,8192]{0,1:T(8,128)(4,1)S(1)} %fusion.7, bf16[8192,128]{0,1:T(8,128)(2,1)} %all-gather.7.cloned.1.call-done, f32[5,128]{1,0:T(8,128)S(1)} %fusion.1), kind=kOutput, calls=%fused_computation.18 | convolution fusion | flops 1368555520 | bytes 24286208 | tf_op jit(solution)/shard_map/kgtp,pkd->kgtd/dot_general | solution.py:49
  204.4 81.0 %all-gather.9.cloned.1.call-done = bf16[640,5120]{0,1:T(8,128)(2,1)} async-done(((bf16[640,80]{0,1:T(8,128)(2,1)}), bf16[640,5120]{0,1:T(8,128)(2,1)}) %all-gather.9.cloned.1.call-update) | async-done | bytes 6553616 | tf_op jit(solution)/shard_map/all_gather | solution.py:62
  285.3 6.2 %convolution_convert_fusion = bf16[128,5120]{1,0:T(8,128)(2,1)} fusion(bf16[128,640]{0,1:T(8,128)(2,1)S(1)} %bitcast.77, bf16[640,5120]{0,1:T(8,128)(2,1)} %all-gather.9.cloned.1.call-done), kind=kOutput, calls=%fused_computation.9 | convolution fusion | flops 839516160 | bytes 8028160 | tf_op jit(solution)/shard_map/dot_general | solution.py:60
  291.5 0.6 dynamic_slice.14
  292.1 0.6 dynamic_slice.15
  294.1 0.7 iota_compare_fusion.3
  294.7 1.5 bitcast_select_fusion.1
  296.2 86.8 %all-reduce.2.cloned.1.call-done = bf16[128,5120]{1,0:T(8,128)(2,1)} async-done(((bf16[128,5120]{1,0:T(8,128)(2,1)}), bf16[128,5120]{1,0:T(8,128)(2,1)}) %all-reduce.2.cloned.1.call-update) | async-done | bytes 1310736 | tf_op jit(solution)/shard_map/psum | solution.py:66
  383.0 1.6 add_convert_fusion
  (17 shorter events, 0.3 us)
Async XLA Ops:
  7.2 3.9 copy-start
  7.2 126.6 %all-gather.5.cloned.1.call-start = ((), (), s32[]{:S(2)}) async-start(), calls=%async_computation.1 | async-start | bytes 2129920 | tf_op jit(solution)/shard_map/all_gather | solution.py:28
  7.9 183.5 %all-gather.7.cloned.1.call-start = ((), (), s32[]{:S(2)}) async-start(), calls=%async_computation.2 | async-start | bytes 2129920 | tf_op jit(solution)/shard_map/all_gather | solution.py:29
  9.5 275.9 %all-gather.9.cloned.1.call-start = ((), (), s32[]{:S(2)}) async-start(), calls=%async_computation.3 | async-start | bytes 6656000 | tf_op jit(solution)/shard_map/all_gather | solution.py:62
  13.1 281.6 %all-to-all-start = ((bf16[2,2,64,16,128]{4,3,1,0,2:T(8,128)(2,1)}), bf16[2,2,64,16,128]{4,3,1,0,2:T(8,128)(2,1)S(1)}, u32[]{:S(2)}, u32[]{:S(2)}) async-start(bf16[2,2,64,16,128]{4,3,1,0,2:T(8,128)(2,1)} %select_bitcast_fusion), calls=%async_computation | async-start | bytes 2097152 | tf_op jit(solution)/shard_map/all_to_all | solution.py:89
  29.5 353.5 %all-reduce.2.cloned.1.call-start = ((), (), s32[]{:S(2)}) async-start(), calls=%async_computation.4 | async-start | bytes 2621440 | tf_op jit(solution)/shard_map/psum | solution.py:66
  138.6 7.0 %copy-start.1 = (f32[8192,128,5]{1,0,2:T(8,128)}, f32[8192,128,5]{1,0,2:T(8,128)S(1)}, u32[]{:S(2)}) copy-start(f32[8192,128,5]{1,0,2:T(8,128)S(1)} %get-tuple-element.7) | copy-start | bytes 62914564
  204.3 178.7 %copy-start.2 = (bf16[128,640]{1,0:T(8,128)(2,1)S(1)}, bf16[128,640]{1,0:T(8,128)(2,1)}, u32[]{:S(2)}) copy-start(bf16[128,640]{1,0:T(8,128)(2,1)} %param.13) | copy-start | bytes 491524
Sparse Core Ops, SparseCore 0:
  11.3 100.3 all-gather.4
  115.5 75.8 all-gather.6
  194.7 90.5 all-gather.8
  291.6 91.3 all-reduce.1
where the time goes:
time: 392 us; the launch traced here: 391 us
  waiting for transfers between devices  210 us (54%)
  blocking collectives  98.7 us (25%)
  matrix products  23.8 us (6%)
  starting transfers between devices  16.6 us (4%)
  other arithmetic  15.4 us (4%)
  between operations  15.2 us (4%)
  local copies, waits for them, and re-layouts  11.5 us (3%)
    all_gather x1, blocking collectives, on_device(): segment_part = lax.all_gather(stretch_segments, 'seq', axis=0, tiled=True)  98.7 us
    psum x1, waiting for transfers between devices, on_device(): lax.psum(partial_value.astype(jnp.bfloat16), 'head').astype(jnp.float32)  86.8 us
    all_gather x1, waiting for transfers between devices, on_device(): lax.all_gather(out_weight, 'seq', axis=1, tiled=True)  81 us
    all_gather x1, waiting for transfers between devices, on_device(): value_part = lax.all_gather(block_value_rows, 'seq', axis=0, tiled=True)  40.7 us
    all_to_all x1, starting transfers between devices, on_device(): lax.all_to_all(outgoing, 'seq', split_axis=2, concat_axis=2, tiled=True)  16.5 us
    dot_general x1, matrix products, on_device(): jnp.einsum('kgtp,pkd->kgtd', weights.astype(jnp.bfloat16), value_three, p...  12.9 us
    unnamed x8, local copies, waits for them, and re-layouts  9.51 us
  transfers between devices with their start and end apart: 5, of which 3 were waited for; matrix products, arithmetic and copies ran while one was open for 11% of the time, Pallas kernels for 0%

commit v1 on v0

--- a/solution.py
+++ b/solution.py
@@ -63,7 +63,10 @@
         preferred_element_type=jnp.float32,
     )
     feature_width = partial_value.shape[1] // lax.axis_size("head")
-    total = lax.psum(partial_value.astype(jnp.bfloat16), "head").astype(jnp.float32)
+    deliver_classes_now = lambda in_array: jax.lax.all_gather(in_array, axis_name="head").sum(
+        axis=0
+    )
+    total = deliver_classes_now(partial_value.astype(jnp.bfloat16)).astype(jnp.float32)
     mine = lax.dynamic_slice_in_dim(total, lax.axis_index("head") * feature_width, feature_width, 1)
     layer_out = (residual.astype(jnp.float32) + mine).astype(jnp.bfloat16)
     local_pages = cache_by_prefill.shape[2]

time: 392 us -> 528 us (1.35)
  the two profiles are of different devices: /device:TPU:16 before, /device:TPU:56 now
where the time goes in v1:
time: 528 us; the launch traced here: 527 us
  waiting for transfers between devices  367 us (70%)
  blocking collectives  81.5 us (15%)
  matrix products  23.8 us (5%)
  other arithmetic  19.6 us (4%)
  between operations  15.2 us (3%)
  local copies, waits for them, and re-layouts  11.6 us (2%)
  starting transfers between devices  8.63 us (2%)
    all_gather x1, waiting for transfers between devices, on_device(): jax.lax.all_gather(in_array, axis_name='head').sum(axis=0)  184 us
    all_gather x1, waiting for transfers between devices, on_device(): lax.all_gather(out_weight, 'seq', axis=1, tiled=True)  83.1 us
    all_gather x1, blocking collectives, on_device(): segment_part = lax.all_gather(stretch_segments, 'seq', axis=0, tiled=True)  81.5 us
    all_gather x1, waiting for transfers between devices, on_device(): value_part = lax.all_gather(block_value_rows, 'seq', axis=0, tiled=True)  61.9 us
    all_to_all x1, waiting for transfers between devices, on_device(): lax.all_to_all(outgoing, 'seq', split_axis=2, concat_axis=2, tiled=True)  34.4 us
    dot_general x1, matrix products, on_device(): jnp.einsum('kgtp,pkd->kgtd', weights.astype(jnp.bfloat16), value_three, p...  12.9 us
  transfers between devices with their start and end apart: 5, of which 5 were waited for; matrix products, arithmetic and copies ran while one was open for 7% of the time, Pallas kernels for 0%

profile of v1, /device:TPU:56, one launch (start us, length us, event | category | flops | bytes accessed | tf_op | source)
XLA Modules:
  0.0 527.2 jit_solution(7376060378971228269)
XLA Ops:
  7.2 0.7 all-gather.7.cloned.1.call-update
  8.0 1.5 copy.27
  9.5 0.7 all-gather.11.cloned.1.call-update
  10.2 1.1 copy.25
  11.3 81.5 %all-gather.1 = s32[64,1,128]{2,1,0:T(1,128)S(1)} all-gather(s32[1,1,128]{2,1,0:T(1,128)} %bitcast.81), channel_id=1, replica_groups=mesh['seq'=64,'head'=8] {'seq'}, dimensions={0}, use_global_device_ids=true | all-gather | bytes 33280 | tf_op jit(solution)/shard_map/all_gather | solution.py:30
  92.8 4.4 fusion.7
  97.2 1.9 all-gather.7.cloned.1.call-done
  99.2 4.7 fusion
  103.9 7.0 %copy-done.1 = f32[8192,128,5]{1,0,2:T(8,128)} copy-done((f32[8192,128,5]{1,0,2:T(8,128)}, f32[8192,128,5]{1,0,2:T(8,128)S(1)}, u32[]{:S(2)}) %copy-start.1) | copy-done | bytes 20971544
  110.9 5.2 fusion.1
  116.1 61.9 %all-gather.9.cloned.1.call-done = bf16[8192,128]{0,1:T(8,128)(2,1)} async-done(((bf16[128,128]{0,1:T(8,128)(2,1)}), bf16[8192,128]{0,1:T(8,128)(2,1)}) %all-gather.9.cloned.1.call-update) | async-done | bytes 2097168 | tf_op jit(solution)/shard_map/all_gather | solution.py:29
  178.0 12.9 %fusion.16 = bf16[5,128,128]{1,2,0:T(8,128)(2,1)S(1)} fusion(f32[8192,128,5]{1,0,2:T(8,128)} %copy-done.1, f32[5,128]{1,0:T(8,128)S(1)} %broadcast_maximum_fusion, pred[128,8192]{0,1:T(8,128)(4,1)S(1)} %fusion.7, bf16[8192,128]{0,1:T(8,128)(2,1)} %all-gather.9.cloned.1.call-done, f32[5,128]{1,0:T(8,128)S(1)} %fusion.1), kind=kOutput, calls=%fused_computation.18 | convolution fusion | flops 1368555520 | bytes 24286208 | tf_op jit(solution)/shard_map/kgtp,pkd->kgtd/dot_general | solution.py:49
  190.9 83.1 %all-gather.11.cloned.1.call-done = bf16[640,5120]{0,1:T(8,128)(2,1)} async-done(((bf16[640,80]{0,1:T(8,128)(2,1)}), bf16[640,5120]{0,1:T(8,128)(2,1)}) %all-gather.11.cloned.1.call-update) | async-done | bytes 6553616 | tf_op jit(solution)/shard_map/all_gather | solution.py:62
  274.0 6.2 %convolution_convert_fusion = bf16[128,5120]{1,0:T(8,128)(2,1)} fusion(bf16[128,640]{0,1:T(8,128)(2,1)S(1)} %bitcast.79, bf16[640,5120]{0,1:T(8,128)(2,1)} %all-gather.11.cloned.1.call-done), kind=kOutput, calls=%fused_computation.9 | convolution fusion | flops 839516160 | bytes 8028160 | tf_op jit(solution)/shard_map/dot_general | solution.py:60
  280.4 0.8 gather_fusion
  281.2 1.2 select_bitcast_fusion
  282.4 8.5 %all-to-all-start = ((bf16[2,2,64,16,128]{4,3,1,0,2:T(8,128)(2,1)}), bf16[2,2,64,16,128]{4,3,1,0,2:T(8,128)(2,1)S(1)}, u32[]{:S(2)}, u32[]{:S(2)}) async-start(bf16[2,2,64,16,128]{4,3,1,0,2:T(8,128)(2,1)} %select_bitcast_fusion), calls=%async_computation | async-start | bytes 2097152 | tf_op jit(solution)/shard_map/all_to_all | solution.py:92
  291.5 0.6 dynamic_slice.15
  293.4 0.7 iota_compare_fusion.3
  294.0 34.4 %all-to-all-done = bf16[2,2,64,16,128]{4,3,1,0,2:T(8,128)(2,1)S(1)} async-done(((bf16[2,2,64,16,128]{4,3,1,0,2:T(8,128)(2,1)}), bf16[2,2,64,16,128]{4,3,1,0,2:T(8,128)(2,1)S(1)}, u32[]{:S(2)}, u32[]{:S(2)}) %all-to-all-start) | async-done | bytes 1048608 | tf_op jit(solution)/shard_map/all_to_all | solution.py:92
  328.5 1.5 bitcast_select_fusion.1
  330.0 184.1 %all-gather.13.cloned.1.call-done = bf16[1024,5120]{1,0:T(8,128)(2,1)} async-done(((bf16[128,5120]{1,0:T(8,128)(2,1)}), bf16[1024,5120]{1,0:T(8,128)(2,1)}) %all-gather.13.cloned.1.call-update) | async-done | bytes 10485776 | tf_op jit(solution)/shard_map/all_gather | solution.py:66
  514.1 5.8 %reduce_sum.44 = bf16[128,5120]{1,0:T(8,128)(2,1)S(1)} reduce(bf16[8,128,5120]{2,1,0:T(8,128)(2,1)} %bitcast.76, bf16[]{:T(256)} %constant.79.clone.1), dimensions={0}, to_apply=%region_2.3 | reduce | flops 4587520 | bytes 11796482 | tf_op jit(solution)/shard_map/reduce_sum | solution.py:66
  520.0 0.7 add_convert_fusion
  (22 shorter events, 1.0 us)
Async XLA Ops:
  7.2 273.2 %copy-start = (bf16[2,2,32,16,128]{4,3,2,1,0:T(8,128)(2,1)S(1)}, bf16[2,2,32,16,128]{4,3,2,1,0:T(8,128)(2,1)}, u32[]{:S(2)}) copy-start(bf16[2,2,32,16,128]{4,3,2,1,0:T(8,128)(2,1)} %param.15) | copy-start | bytes 1572868
  7.2 92.0 %all-gather.7.cloned.1.call-start = ((), (), s32[]{:S(2)}) async-start(), calls=%async_computation.1 | async-start | bytes 2129920 | tf_op jit(solution)/shard_map/all_gather | solution.py:28
  7.9 170.0 %all-gather.9.cloned.1.call-start = ((), (), s32[]{:S(2)}) async-start(), calls=%async_computation.2 | async-start | bytes 2129920 | tf_op jit(solution)/shard_map/all_gather | solution.py:29
  9.5 264.5 %all-gather.11.cloned.1.call-start = ((), (), s32[]{:S(2)}) async-start(), calls=%async_computation.3 | async-start | bytes 6656000 | tf_op jit(solution)/shard_map/all_gather | solution.py:62
  10.2 503.9 %all-gather.13.cloned.1.call-start = ((), (), s32[]{:S(2)}) async-start(), calls=%async_computation.4 | async-start | bytes 11796480 | tf_op jit(solution)/shard_map/all_gather | solution.py:66
  103.9 7.0 %copy-start.1 = (f32[8192,128,5]{1,0,2:T(8,128)}, f32[8192,128,5]{1,0,2:T(8,128)S(1)}, u32[]{:S(2)}) copy-start(f32[8192,128,5]{1,0,2:T(8,128)S(1)} %get-tuple-element.7) | copy-start | bytes 62914564
  116.1 164.1 %copy-start.3 = (s32[128]{0:T(128)S(1)}, s32[128]{0:T(128)}, u32[]{:S(2)}) copy-start(s32[128]{0:T(128)} %param.16) | copy-start | bytes 1540
  116.1 164.1 %copy-start.4 = (s32[128]{0:T(128)S(1)}, s32[128]{0:T(128)}, u32[]{:S(2)}) copy-start(s32[128]{0:T(128)} %param.17) | copy-start | bytes 1540
  280.1 239.8 %copy-start.2 = (bf16[128,640]{1,0:T(8,128)(2,1)S(1)}, bf16[128,640]{1,0:T(8,128)(2,1)}, u32[]{:S(2)}) copy-start(bf16[128,640]{1,0:T(8,128)(2,1)} %param.13) | copy-start | bytes 491524
  282.4 46.1 %all-to-all-start = ((bf16[2,2,64,16,128]{4,3,1,0,2:T(8,128)(2,1)}), bf16[2,2,64,16,128]{4,3,1,0,2:T(8,128)(2,1)S(1)}, u32[]{:S(2)}, u32[]{:S(2)}) async-start(bf16[2,2,64,16,128]{4,3,1,0,2:T(8,128)(2,1)} %select_bitcast_fusion), calls=%async_computation | async-start | bytes 2097152 | tf_op jit(solution)/shard_map/all_to_all | solution.py:92
Sparse Core Ops, SparseCore 0:
  11.3 87.7 all-gather.6
  103.0 74.9 all-gather.8
  181.2 92.6 all-gather.10
  280.3 233.7 all-gather.12
